TPU v7x, 32 devices: a whole 2x2x4 slice. The times are simulated.
32 devices in a mesh: group: 2 (over y), tile: 4 (over z), sect: 2 (over x), sub: 2 (over core).
Axes of the slice: x: 2, y: 2, z: 4, core: 2. Of those that a mesh axis runs over, the one named last changes fastest.
Arguments:
- air_state: float32 [4, 80, 64, 256], P(None, ('sect', 'sub'), ('group', 'tile')), parts along dimension 2, may hold values from -3 to 3
- fire_level: float32 [640, 2560], P(('group', 'tile'), ('sect', 'sub')), parts along dimension 0, may hold values from 0.2 to 3
- fuel_left: float32 [640, 2560], P(('group', 'tile'), ('sect', 'sub')), parts along dimension 0, may hold values from 0.3 to 1
- fuel_class: int32 [640, 2560], P(('group', 'tile'), ('sect', 'sub')), parts along dimension 0, may hold values from 0 to 12
- ignition: int32 [640, 2560], P(('group', 'tile'), ('sect', 'sub')), parts along dimension 0, may hold values from 0 to 4, as said below
- plan: int32 [4], replicated, may hold values from 1 to 3
- spread_rate: float32 [13], replicated, may hold values from 0.05 to 0.3
- burn_time: float32 [13], replicated, may hold values from 0.5 to 8
- heat_content: float32 [13], replicated, may hold values from 1 to 10
- moisture_content: float32 [13], replicated, may hold values from 0.1 to 1
Outputs:
- air_out: float32 [4, 80, 64, 256], P(None, ('sect', 'sub'), ('group', 'tile')), parts along dimension 2
- level_out: float32 [640, 2560], P(('group', 'tile'), ('sect', 'sub')), parts along dimension 0
- fuel_out: float32 [640, 2560], P(('group', 'tile'), ('sect', 'sub')), parts along dimension 0
There are 2 independent parts, one for each index of `group`. A program takes and returns all parts, laid end to end along the dimension named above; an argument that names none is the same for every part. Nothing has to cross between parts.
Inputs may be any that keep to these rules, and one draw needn't show every extreme that they name: `ignition`: A cell with value c is ignited at the start of coupling step c; cells with value 4 are not ignited in the window. Ignited cells lie in scattered atmosphere columns. The plan is shared by all scenarios.
All inputs are finite; a program needn't handle non-finite values.
Results may differ from a plain program's by a relative error of at most 0.0001.
Values sent between devices are 32-bit elements; how exact they have to be, the bound alone decides.
A program may use at most 128 MiB of HBM per device.

v0:
```python
import jax
import jax.numpy as jnp
from jax import lax
from jax.sharding import PartitionSpec as P

LEVELS = 80
REFINE = 10
STEPS = 4
SUBSTEPS = 4


air_delta = 0.1
diffusion = 0.2
heat_gain = 20.0
vapour_gain = 20.0
lift_gain = 0.3
wind_gain = 0.5
fire_delta = 0.15


def padded_2(block, sides, width):
    for axis, dim in sides:
        count = lax.axis_size(axis)
        forward = [(i, i + 1) for i in range(count - 1)]
        backward = [(target, source) for source, target in forward]
        low = lax.ppermute(
            lax.slice_in_dim(block, block.shape[dim] - width, None, axis=dim), axis, forward
        )
        high = lax.ppermute(lax.slice_in_dim(block, 0, width, axis=dim), axis, backward)
        block = jnp.concatenate([low, block, high], axis=dim)
    return block


def level_weights(layer_count):
    height = jnp.arange(layer_count).astype(jnp.float32)
    profile = jnp.exp(-2.0 * height / layer_count)
    profile = layer_count * profile / jnp.sum(profile)
    column = jnp.exp(-height / layer_count)
    column = column / jnp.sum(column)
    return (profile, column)


def lookup(tables, classes):
    result = jnp.zeros((tables.shape[0],) + classes.shape, jnp.float32)
    for category in range(tables.shape[1]):
        result = jnp.where((classes == category)[None], tables[:, category][:, None, None], result)
    return result


def mend_edges(padded, at_start, at_end, axis_dim):
    extent = padded.shape[axis_dim]
    leading = lax.slice_in_dim(padded, 0, 1, axis=axis_dim)
    following = lax.slice_in_dim(padded, 1, 2, axis=axis_dim)
    interior = lax.slice_in_dim(padded, 1, extent - 1, axis=axis_dim)
    preceding = lax.slice_in_dim(padded, extent - 2, extent - 1, axis=axis_dim)
    trailing = lax.slice_in_dim(padded, extent - 1, extent, axis=axis_dim)
    return jnp.concatenate(
        [jnp.where(at_start, following, leading), interior, jnp.where(at_end, preceding, trailing)],
        axis=axis_dim,
    )


def advance_level(padded, rate_cell, wind_east, wind_north, fire_step):
    at_centre = padded[1:-1, 1:-1]
    at_west = padded[:-2, 1:-1]
    at_east = padded[2:, 1:-1]
    at_south = padded[1:-1, :-2]
    at_north = padded[1:-1, 2:]
    steepness = jnp.sqrt(
        jnp.maximum(at_centre - at_west, 0.0) ** 2
        + jnp.minimum(at_east - at_centre, 0.0) ** 2
        + jnp.maximum(at_centre - at_south, 0.0) ** 2
        + jnp.minimum(at_north - at_centre, 0.0) ** 2
    )
    grad_east = 0.5 * (at_east - at_west)
    grad_north = 0.5 * (at_north - at_south)
    tailwind = (wind_east * grad_east + wind_north * grad_north) / jnp.sqrt(
        grad_east * grad_east + grad_north * grad_north + 1.0
    )
    fire_speed = rate_cell * (1.0 + wind_gain * jnp.maximum(tailwind, 0.0))
    return at_centre - fire_step * fire_speed * steepness


def burn_fuel(level_set, fuel_now, energy, vapour, burnout, heat_cell, moist_cell, fire_step):
    burning = jnp.clip(0.5 - level_set, 0.0, 1.0)
    remain = fuel_now * jnp.exp(-fire_step * burning / burnout)
    consumed = fuel_now - remain
    return (remain, energy + consumed * heat_cell, vapour + consumed * moist_cell)


def fire_core(
    padded,
    fuel_now,
    energy,
    vapour,
    rate_cell,
    burnout,
    heat_cell,
    moist_cell,
    wind_east,
    wind_north,
    fire_step,
):
    level_set = advance_level(padded, rate_cell, wind_east, wind_north, fire_step)
    remain, energy, vapour = burn_fuel(
        level_set, fuel_now, energy, vapour, burnout, heat_cell, moist_cell, fire_step
    )
    return (level_set, remain, energy, vapour)


def air_core(padded, flux_coarse, profile):
    at_centre = padded[:, 1:-1, 1:-1, 1:-1]
    at_below = padded[:, :-2, 1:-1, 1:-1]
    at_above = padded[:, 2:, 1:-1, 1:-1]
    at_west = padded[:, 1:-1, :-2, 1:-1]
    at_east = padded[:, 1:-1, 2:, 1:-1]
    at_south = padded[:, 1:-1, 1:-1, :-2]
    at_north = padded[:, 1:-1, 1:-1, 2:]
    speed_east = at_centre[2]
    speed_north = at_centre[3]
    advect = (
        jnp.maximum(speed_east, 0.0) * (at_centre - at_west)
        + jnp.minimum(speed_east, 0.0) * (at_east - at_centre)
        + jnp.maximum(speed_north, 0.0) * (at_centre - at_south)
        + jnp.minimum(speed_north, 0.0) * (at_north - at_centre)
    )
    diffused = at_west + at_east + at_south + at_north + at_below + at_above - 6.0 * at_centre
    lift_east = at_east[0] + 0.6 * at_east[1] - (at_west[0] + 0.6 * at_west[1])
    lift_north = at_north[0] + 0.6 * at_north[1] - (at_south[0] + 0.6 * at_south[1])
    heights = profile[:, None, None]
    forcing = jnp.stack(
        [
            heat_gain * flux_coarse[0][None] * heights,
            vapour_gain * flux_coarse[1][None] * heights,
            0.5 * lift_gain * lift_east,
            0.5 * lift_gain * lift_north,
        ]
    )
    return at_centre + air_delta * (diffusion * diffused - advect + forcing)


def coarsen(fine_field, refine_by):
    channels, row_count, col_count = fine_field.shape
    blocks = fine_field.reshape(
        channels, row_count // refine_by, refine_by, col_count // refine_by, refine_by
    )
    return jnp.sum(blocks, axis=(2, 4)) / (refine_by * refine_by)


def local(
    air_state,
    fire_level,
    fuel_left,
    fuel_class,
    ignition,
    plan,
    spread_rate,
    burn_time,
    heat_content,
    moisture_content,
):
    tables = jnp.stack([spread_rate, burn_time, heat_content, moisture_content])
    cell_values = lookup(tables, fuel_class)
    rate_cell = cell_values[0]
    burnout = cell_values[1]
    heat_cell = cell_values[2]
    moist_cell = cell_values[3]
    profile, column = level_weights(LEVELS)
    tile_at = lax.axis_index("tile")
    tile_count = lax.axis_size("tile")
    band_at = lax.axis_index(("sect", "sub"))
    band_count = lax.axis_size(("sect", "sub"))
    tile_first = tile_at == 0
    tile_final = tile_at == tile_count - 1
    band_first = band_at == 0
    band_final = band_at == band_count - 1
    air_field = air_state
    local_depth = air_state.shape[1]
    offset = band_at * local_depth
    profile_part = lax.dynamic_slice_in_dim(profile, offset, local_depth)
    column_part = lax.dynamic_slice_in_dim(column, offset, local_depth)
    level_set = fire_level
    fuel_now = fuel_left
    for coupling in range(STEPS):
        partial_value = jnp.sum(column_part[None, :, None, None] * air_field[2:4], axis=1)
        wind_coarse = lax.psum_scatter(
            partial_value, ("sect", "sub"), scatter_dimension=2, tiled=True
        )
        wind_fine = jnp.repeat(jnp.repeat(wind_coarse, REFINE, axis=1), REFINE, axis=2)
        fire_step = plan[coupling].astype(jnp.float32) * fire_delta
        level_set = jnp.where(ignition <= coupling, jnp.minimum(level_set, -1.0), level_set)
        energy = jnp.zeros_like(level_set)
        vapour = jnp.zeros_like(level_set)
        for sub_step in range(SUBSTEPS):
            padded = padded_2(level_set, (("tile", 0), (("sect", "sub"), 1)), 1)
            padded = mend_edges(padded, tile_first, tile_final, 0)
            padded = mend_edges(padded, band_first, band_final, 1)
            level_set, fuel_now, energy, vapour = fire_core(
                padded,
                fuel_now,
                energy,
                vapour,
                rate_cell,
                burnout,
                heat_cell,
                moist_cell,
                wind_fine[0],
                wind_fine[1],
                fire_step,
            )
        flux_coarse = coarsen(jnp.stack([energy, vapour]), REFINE)
        flux_whole = lax.all_gather(flux_coarse, ("sect", "sub"), axis=2, tiled=True)
        padded_air = padded_2(air_field, (("tile", 2), (("sect", "sub"), 1)), 1)
        padded_air = jnp.pad(padded_air, ((0, 0), (0, 0), (0, 0), (1, 1)))
        air_field = air_core(padded_air, flux_whole, profile_part)
    return (air_field, level_set, fuel_now)


def solution(mesh):
    placed = (
        P(None, ("sect", "sub"), ("group", "tile"), None),
        P(("group", "tile"), ("sect", "sub")),
        P(("group", "tile"), ("sect", "sub")),
        P(("group", "tile"), ("sect", "sub")),
        P(("group", "tile"), ("sect", "sub")),
        P(),
        P(),
        P(),
        P(),
        P(),
    )
    return jax.shard_map(
        local,
        mesh=mesh,
        in_specs=placed,
        out_specs=(
            P(None, ("sect", "sub"), ("group", "tile"), None),
            P(("group", "tile"), ("sect", "sub")),
            P(("group", "tile"), ("sect", "sub")),
        ),
        check_vma=False,
    )
```

profile of v0, /device:TPU:9, one launch (start us, length us, event | category | flops | bytes accessed | tf_op | source)
XLA Modules:
  0.0 516.4 jit_solution(6921379794625309916)
XLA Ops:
  19.9 4.2 collective-permute-start.6
  30.9 7.7 %reduce-scatter.13.cloned.1.call-done = f32[64,16]{1,0:T(8,128)} async-done(((f32[256,16]{1,0:T(8,128)}), f32[64,16]{1,0:T(8,128)}) %reduce-scatter.13.cloned.1.call-update) | async-done | bytes 4112
  51.0 4.7 collective-permute-start.10
  103.3 3.5 collective-permute-start.25
  108.5 3.6 stack.85
  113.8 3.6 stack.84
  120.5 4.7 all_gather.12
  125.6 3.7 collective-permute-start.26
  148.6 16.1 %reduce-scatter.15.cloned.1.call-done = f32[64,16]{1,0:T(8,128)} async-done(((f32[256,16]{1,0:T(8,128)}), f32[64,16]{1,0:T(8,128)}) %reduce-scatter.15.cloned.1.call-update) | async-done | bytes 4112
  176.1 4.6 collective-permute-start.30
  218.6 3.5 collective-permute-start.21
  229.6 4.3 stack.89
  236.4 4.3 stack.88
  243.6 7.3 %all_gather.13 = f32[2,8,256]{1,0,2:T(2,128)S(1)} all-gather(f32[2,8,64]{1,0,2:T(2,128)S(1)} %copy.237), channel_id=1, replica_groups=mesh['group'=2,'tile'=4,'sect'=2,'sub'=2] {'sect','sub'}, dimensions={2}, use_global_device_ids=true | all-gather | bytes 20480 | tf_op jit(solution)/shard_map/all_gather | solution.py:212
  272.9 16.6 %reduce-scatter.17.cloned.1.call-done = f32[64,16]{1,0:T(8,128)} async-done(((f32[256,16]{1,0:T(8,128)}), f32[64,16]{1,0:T(8,128)}) %reduce-scatter.17.cloned.1.call-update) | async-done | bytes 4112
  302.7 4.6 collective-permute-start.50
  355.3 4.3 stack.93
  362.1 4.3 stack.92
  369.3 7.3 %all_gather.14 = f32[2,8,256]{1,0,2:T(2,128)S(1)} all-gather(f32[2,8,64]{1,0,2:T(2,128)S(1)} %copy.252), channel_id=1, replica_groups=mesh['group'=2,'tile'=4,'sect'=2,'sub'=2] {'sect','sub'}, dimensions={2}, use_global_device_ids=true | all-gather | bytes 20480 | tf_op jit(solution)/shard_map/all_gather | solution.py:212
  398.6 16.6 %reduce-scatter.19.cloned.1.call-done = f32[64,16]{1,0:T(8,128)} async-done(((f32[256,16]{1,0:T(8,128)}), f32[64,16]{1,0:T(8,128)}) %reduce-scatter.19.cloned.1.call-update) | async-done | bytes 4112
  428.3 4.6 collective-permute-start.70
  476.3 4.3 stack.97
  483.2 4.3 stack.96
  490.4 6.8 %all_gather.15 = f32[2,8,256]{1,0,2:T(2,128)S(1)} all-gather(f32[2,8,64]{1,0,2:T(2,128)S(1)} %copy.267), channel_id=1, replica_groups=mesh['group'=2,'tile'=4,'sect'=2,'sub'=2] {'sect','sub'}, dimensions={2}, use_global_device_ids=true | all-gather | bytes 20480 | tf_op jit(solution)/shard_map/all_gather | solution.py:212
  (559 shorter events, 346.8 us)
Async XLA Ops:
  7.2 31.4 %reduce-scatter.13.cloned.1.call-start = ((), (), s32[]{:S(2)}) async-start(), calls=%async_computation.4 | async-start | bytes 163840
  8.3 11.5 %collective-permute-start.4 = (f32[1,640]{1,0:T(1,128)S(1)}, f32[1,640]{1,0:T(1,128)S(1)}, u32[]{:S(2)}, u32[]{:S(2)}) collective-permute-start(f32[1,640]{1,0:T(1,128)S(1)} %get-tuple-element.187), channel_id=1, source_target_pairs={{0,4},{4,8},{8,12},{1,5},{5,9},{9,13},{2,6},{6,10},{10,14},{3,7},{... | collective-permute-start | bytes 7688 | tf_op jit(solution)/shard_map/ppermute | solution.py:26
  17.6 147.1 %reduce-scatter.15.cloned.1.call-start = ((), (), s32[]{:S(2)}) async-start(), calls=%async_computation.5 | async-start | bytes 163840
  62.2 11.8 %collective-permute-start.12 = (f32[1,640]{1,0:T(1,128)S(1)}, f32[1,640]{1,0:T(1,128)S(1)}, u32[]{:S(2)}, u32[]{:S(2)}) collective-permute-start(f32[1,640]{1,0:T(1,128)S(1)} %get-tuple-element.183), channel_id=1, source_target_pairs={{0,4},{4,8},{8,12},{1,5},{5,9},{9,13},{2,6},{6,10},{10,14},{3,7},{... | collective-permute-start | bytes 7688 | tf_op jit(solution)/shard_map/ppermute | solution.py:26
  65.3 8.7 %collective-permute-start.13 = (f32[1,640]{1,0:T(1,128)S(1)}, f32[1,640]{1,0:T(1,128)S(1)}, u32[]{:S(2)}, u32[]{:S(2)}) collective-permute-start(f32[1,640]{1,0:T(1,128)S(1)} %get-tuple-element.184), channel_id=1, source_target_pairs={{4,0},{8,4},{12,8},{5,1},{9,5},{13,9},{6,2},{10,6},{14,10},{7,3},{... | collective-permute-start | bytes 7688 | tf_op jit(solution)/shard_map/ppermute | solution.py:29
  68.1 67.0 %collective-permute-start = (f32[4,20,1,256]{3,1,2,0:T(8,128)}, f32[4,20,1,256]{3,1,2,0:T(8,128)}, u32[]{:S(2)}, u32[]{:S(2)}) collective-permute-start(f32[4,20,1,256]{3,1,2,0:T(8,128)} %get-tuple-element.81), channel_id=1, source_target_pairs={{0,4},{4,8},{8,12},{1,5},{5,9},{9,13},{2,6},{6,10},{10,14},{3,7},{... | collective-permute-start | bytes 245768 | tf_op jit(solution)/shard_map/ppermute | solution.py:26
  71.3 65.1 %collective-permute-start.1 = (f32[4,20,1,256]{3,1,2,0:T(8,128)S(1)}, f32[4,20,1,256]{3,1,2,0:T(8,128)}, u32[]{:S(2)}, u32[]{:S(2)}) collective-permute-start(f32[4,20,1,256]{3,1,2,0:T(8,128)S(1)} %get-tuple-element.80), channel_id=1, source_target_pairs={{4,0},{8,4},{12,8},{5,1},{9,5},{13,9},{6,2},{10,6},{14,10},{7,3},{... | collective-permute-start | bytes 245768 | tf_op jit(solution)/shard_map/ppermute | solution.py:29
  101.1 24.5 %collective-permute-start.24 = (f32[1,640]{1,0:T(1,128)}, f32[1,640]{1,0:T(1,128)S(1)}, u32[]{:S(2)}, u32[]{:S(2)}) collective-permute-start(f32[1,640]{1,0:T(1,128)} %get-tuple-element.179), channel_id=1, source_target_pairs={{0,4},{4,8},{8,12},{1,5},{5,9},{9,13},{2,6},{6,10},{10,14},{3,7},{... | collective-permute-start | bytes 7688 | tf_op jit(solution)/shard_map/ppermute | solution.py:26
  103.3 22.2 %collective-permute-start.25 = (f32[1,640]{1,0:T(1,128)}, f32[1,640]{1,0:T(1,128)S(1)}, u32[]{:S(2)}, u32[]{:S(2)}) collective-permute-start(f32[1,640]{1,0:T(1,128)} %get-tuple-element.180), channel_id=1, source_target_pairs={{4,0},{8,4},{12,8},{5,1},{9,5},{13,9},{6,2},{10,6},{14,10},{7,3},{... | collective-permute-start | bytes 7688 | tf_op jit(solution)/shard_map/ppermute | solution.py:29
  147.8 141.8 %reduce-scatter.17.cloned.1.call-start = ((), (), s32[]{:S(2)}) async-start(), calls=%async_computation.6 | async-start | bytes 163840
  211.0 11.1 %collective-permute-start.38 = (f32[82,1]{1,0:T(8,128)S(1)}, f32[82,1]{1,0:T(8,128)S(1)}, u32[]{:S(2)}, u32[]{:S(2)}) collective-permute-start(f32[82,1]{1,0:T(8,128)S(1)} %get-tuple-element.141), channel_id=1, source_target_pairs={{0,1},{1,2},{2,3},{4,5},{5,6},{6,7},{8,9},{9,10},{10,11},{12,13},{... | collective-permute-start | bytes 992 | tf_op jit(solution)/shard_map/ppermute | solution.py:26
  216.7 44.4 %collective-permute-start.20 = (f32[4,20,1,256]{3,1,2,0:T(8,128)}, f32[4,20,1,256]{3,1,2,0:T(8,128)S(1)}, u32[]{:S(2)}, u32[]{:S(2)}) collective-permute-start(f32[4,20,1,256]{3,1,2,0:T(8,128)} %get-tuple-element.74), channel_id=1, source_target_pairs={{0,4},{4,8},{8,12},{1,5},{5,9},{9,13},{2,6},{6,10},{10,14},{3,7},{... | collective-permute-start | bytes 245768 | tf_op jit(solution)/shard_map/ppermute | solution.py:26
  218.6 42.5 %collective-permute-start.21 = (f32[4,20,1,256]{3,1,2,0:T(8,128)}, f32[4,20,1,256]{3,1,2,0:T(8,128)S(1)}, u32[]{:S(2)}, u32[]{:S(2)}) collective-permute-start(f32[4,20,1,256]{3,1,2,0:T(8,128)} %get-tuple-element.75), channel_id=1, source_target_pairs={{4,0},{8,4},{12,8},{5,1},{9,5},{13,9},{6,2},{10,6},{14,10},{7,3},{... | collective-permute-start | bytes 245768 | tf_op jit(solution)/shard_map/ppermute | solution.py:29
  223.3 28.0 %collective-permute-start.44 = (f32[1,640]{1,0:T(1,128)S(1)}, f32[1,640]{1,0:T(1,128)S(1)}, u32[]{:S(2)}, u32[]{:S(2)}) collective-permute-start(f32[1,640]{1,0:T(1,128)S(1)} %get-tuple-element.171), channel_id=1, source_target_pairs={{0,4},{4,8},{8,12},{1,5},{5,9},{9,13},{2,6},{6,10},{10,14},{3,7},{... | collective-permute-start | bytes 7688 | tf_op jit(solution)/shard_map/ppermute | solution.py:26
  225.2 26.1 %collective-permute-start.45 = (f32[1,640]{1,0:T(1,128)S(1)}, f32[1,640]{1,0:T(1,128)S(1)}, u32[]{:S(2)}, u32[]{:S(2)}) collective-permute-start(f32[1,640]{1,0:T(1,128)S(1)} %get-tuple-element.172), channel_id=1, source_target_pairs={{4,0},{8,4},{12,8},{5,1},{9,5},{13,9},{6,2},{10,6},{14,10},{7,3},{... | collective-permute-start | bytes 7688 | tf_op jit(solution)/shard_map/ppermute | solution.py:29
  272.6 142.6 %reduce-scatter.19.cloned.1.call-start = ((), (), s32[]{:S(2)}) async-start(), calls=%async_computation.7 | async-start | bytes 163840
  337.5 10.9 %collective-permute-start.58 = (f32[82,1]{1,0:T(8,128)S(1)}, f32[82,1]{1,0:T(8,128)S(1)}, u32[]{:S(2)}, u32[]{:S(2)}) collective-permute-start(f32[82,1]{1,0:T(8,128)S(1)} %get-tuple-element.133), channel_id=1, source_target_pairs={{0,1},{1,2},{2,3},{4,5},{5,6},{6,7},{8,9},{9,10},{10,11},{12,13},{... | collective-permute-start | bytes 992 | tf_op jit(solution)/shard_map/ppermute | solution.py:26
  343.2 43.6 %collective-permute-start.40 = (f32[4,20,1,256]{3,1,2,0:T(8,128)}, f32[4,20,1,256]{3,1,2,0:T(8,128)S(1)}, u32[]{:S(2)}, u32[]{:S(2)}) collective-permute-start(f32[4,20,1,256]{3,1,2,0:T(8,128)} %get-tuple-element.67), channel_id=1, source_target_pairs={{0,4},{4,8},{8,12},{1,5},{5,9},{9,13},{2,6},{6,10},{10,14},{3,7},{... | collective-permute-start | bytes 245768 | tf_op jit(solution)/shard_map/ppermute | solution.py:26
  345.1 41.7 %collective-permute-start.41 = (f32[4,20,1,256]{3,1,2,0:T(8,128)}, f32[4,20,1,256]{3,1,2,0:T(8,128)S(1)}, u32[]{:S(2)}, u32[]{:S(2)}) collective-permute-start(f32[4,20,1,256]{3,1,2,0:T(8,128)} %get-tuple-element.68), channel_id=1, source_target_pairs={{4,0},{8,4},{12,8},{5,1},{9,5},{13,9},{6,2},{10,6},{14,10},{7,3},{... | collective-permute-start | bytes 245768 | tf_op jit(solution)/shard_map/ppermute | solution.py:29
  349.6 27.3 %collective-permute-start.64 = (f32[1,640]{1,0:T(1,128)S(1)}, f32[1,640]{1,0:T(1,128)S(1)}, u32[]{:S(2)}, u32[]{:S(2)}) collective-permute-start(f32[1,640]{1,0:T(1,128)S(1)} %get-tuple-element.163), channel_id=1, source_target_pairs={{0,4},{4,8},{8,12},{1,5},{5,9},{9,13},{2,6},{6,10},{10,14},{3,7},{... | collective-permute-start | bytes 7688 | tf_op jit(solution)/shard_map/ppermute | solution.py:26
  351.6 25.4 %collective-permute-start.65 = (f32[1,640]{1,0:T(1,128)S(1)}, f32[1,640]{1,0:T(1,128)S(1)}, u32[]{:S(2)}, u32[]{:S(2)}) collective-permute-start(f32[1,640]{1,0:T(1,128)S(1)} %get-tuple-element.164), channel_id=1, source_target_pairs={{4,0},{8,4},{12,8},{5,1},{9,5},{13,9},{6,2},{10,6},{14,10},{7,3},{... | collective-permute-start | bytes 7688 | tf_op jit(solution)/shard_map/ppermute | solution.py:29
  463.2 10.9 %collective-permute-start.78 = (f32[82,1]{1,0:T(8,128)S(1)}, f32[82,1]{1,0:T(8,128)S(1)}, u32[]{:S(2)}, u32[]{:S(2)}) collective-permute-start(f32[82,1]{1,0:T(8,128)S(1)} %get-tuple-element.125), channel_id=1, source_target_pairs={{0,1},{1,2},{2,3},{4,5},{5,6},{6,7},{8,9},{9,10},{10,11},{12,13},{... | collective-permute-start | bytes 992 | tf_op jit(solution)/shard_map/ppermute | solution.py:26
  468.8 28.8 %collective-permute-start.60 = (f32[4,20,1,256]{3,1,2,0:T(8,128)}, f32[4,20,1,256]{3,1,2,0:T(8,128)S(1)}, u32[]{:S(2)}, u32[]{:S(2)}) collective-permute-start(f32[4,20,1,256]{3,1,2,0:T(8,128)} %get-tuple-element.60), channel_id=1, source_target_pairs={{0,4},{4,8},{8,12},{1,5},{5,9},{9,13},{2,6},{6,10},{10,14},{3,7},{... | collective-permute-start | bytes 245768 | tf_op jit(solution)/shard_map/ppermute | solution.py:26
  470.7 26.9 %collective-permute-start.61 = (f32[4,20,1,256]{3,1,2,0:T(8,128)S(1)}, f32[4,20,1,256]{3,1,2,0:T(8,128)S(1)}, u32[]{:S(2)}, u32[]{:S(2)}) collective-permute-start(f32[4,20,1,256]{3,1,2,0:T(8,128)S(1)} %get-tuple-element.61), channel_id=1, source_target_pairs={{4,0},{8,4},{12,8},{5,1},{9,5},{13,9},{6,2},{10,6},{14,10},{7,3},{... | collective-permute-start | bytes 245768 | tf_op jit(solution)/shard_map/ppermute | solution.py:29
  (99 other events, 705.7 us)
Sparse Core Ops, SparseCore 0:
  17.7 20.8 reduce-scatter.12
  147.9 16.7 reduce-scatter.14
  272.8 16.7 reduce-scatter.16
  398.4 16.7 reduce-scatter.18
where the time goes:
time: 525 us; the launch traced here: 516 us
  starting transfers between devices  215 us (41%)
  waiting for transfers between devices  127 us (24%)
  local copies, waits for them, and re-layouts  85.8 us (16%)
  other arithmetic  42.7 us (8%)
  blocking collectives  26.2 us (5%)
  between operations  19.8 us (4%)
    ppermute x40, starting transfers between devices, padded_2(): lax.ppermute(lax.slice_in_dim(block, block.shape[dim] - width, None, axis...  119 us
    ppermute x40, starting transfers between devices, padded_2(): lax.ppermute(lax.slice_in_dim(block, 0, width, axis=dim), axis, backward)  96 us
    ppermute x40, waiting for transfers between devices, padded_2(): lax.ppermute(lax.slice_in_dim(block, 0, width, axis=dim), axis, backward)  69.9 us
    unnamed x8, waiting for transfers between devices  57.1 us
    another operation x16, local copies, waits for them, and re-layouts, local(): flux_coarse = coarsen(jnp.stack([energy, vapour]), REFINE)  51.9 us
    all_gather x4, blocking collectives, local(): lax.all_gather(flux_coarse, ('sect', 'sub'), axis=2, tiled=True)  26.2 us
    broadcast_in_dim x24, local copies, waits for them, and re-layouts, local(): jnp.repeat(jnp.repeat(wind_coarse, REFINE, axis=1), REFINE, axis=2)  12 us
    unnamed x102, local copies, waits for them, and re-layouts  11.6 us
  transfers between devices with their start and end apart: 84, of which 32 were waited for; matrix products, arithmetic and copies ran while one was open for 16% of the time, Pallas kernels for 0%

commit v1 on v0

v1 whole, which is shorter than its diff:
```python
import functools
import math

import jax
import jax.numpy as jnp
from jax import lax
from jax.experimental import pallas as pl
from jax.experimental.pallas import tpu as pltpu
from jax.sharding import PartitionSpec as P

LEVELS = 80
REFINE = 10
NFUEL = 13
STEPS = 4
SUBSTEPS = 4
HALO = STEPS * SUBSTEPS
HIGH = lax.Precision.HIGHEST
MESH = pl.DeviceIdType.MESH
TINY = 1.1754944e-38
f32 = jnp.float32


def kernel(
    tiles,
    sects,
    subs,
    air_in,
    level_in,
    fuel_in,
    class_in,
    ign_in,
    plan,
    t_rate,
    t_burn,
    t_heat,
    t_moist,
    air_out,
    level_out,
    fuel_out,
    air,
    xh,
    lr,
    side,
    lv,
    bsum,
    binv,
    heat,
    moist,
    ev,
    wind,
    rx,
    ry,
    sx,
    sy,
    wsend,
    wrecv,
    hsend,
    hrecv,
    fsend,
    frecv,
    fire_s,
    fire_r,
    wind_s,
    wind_r,
    flux_s,
    flux_r,
    halo_s,
    halo_r,
):
    bands = sects * subs
    depth = air_in.shape[1]
    width = air_in.shape[3]
    rows, cols = level_in.shape
    full = rows + 2 * HALO
    lanes = cols + 128
    chunks = rows // 8
    all_chunks = full // 8
    coarse = cols // REFINE
    tile_at = lax.axis_index("tile")
    sect_at = lax.axis_index("sect")
    sub_at = lax.axis_index("sub")
    band = sect_at * subs + sub_at
    not_first = tile_at > 0
    not_final = tile_at < tiles - 1
    band_low = band > 0
    band_high = band < bands - 1

    def device(tile_step, at_band):
        return {
            "tile": tile_at + tile_step,
            "sect": at_band // subs,
            "sub": at_band % subs,
        }

    def both(a, b):
        return jnp.logical_and(a, b)

    pending = []

    def send(condition, src, dst, send_sem, recv_sem, where):
        def make():
            return pltpu.make_async_remote_copy(
                src_ref=src,
                dst_ref=dst,
                send_sem=send_sem,
                recv_sem=recv_sem,
                device_id=where,
                device_id_type=MESH,
            )

        @pl.when(condition)
        def _():
            make().start()

        pending.append((condition, make))

    def receive(condition, dst, recv_sem, send_sem, where):
        @pl.when(condition)
        def _():
            pltpu.make_async_remote_copy(
                src_ref=dst,
                dst_ref=dst,
                send_sem=send_sem,
                recv_sem=recv_sem,
                device_id=where,
                device_id_type=MESH,
            ).wait_recv()

    @pl.when(jnp.logical_not(not_first))
    def _():
        hrecv[:, 1] = jnp.zeros_like(hrecv[:, 1])
        lr[:, rows + HALO :, :cols] = jnp.zeros((3, HALO, cols), f32)

        def zero(i, carry):
            for c in range(STEPS):
                for f in range(4):
                    xh[c, 0, f, i] = jnp.zeros((8, width), f32)
            return carry

        lax.fori_loop(0, depth, zero, 0)

    @pl.when(jnp.logical_not(not_final))
    def _():
        hrecv[:, 0] = jnp.zeros_like(hrecv[:, 0])
        lr[:, rows : rows + HALO, :cols] = jnp.zeros((3, HALO, cols), f32)

        def zero(i, carry):
            for c in range(STEPS):
                for f in range(4):
                    xh[c, 1, f, i] = jnp.zeros((8, width), f32)
            return carry

        lax.fori_loop(0, depth, zero, 0)

    @pl.when(jnp.logical_not(band_low))
    def _():
        for c in range(STEPS):
            air[c, :, 0] = jnp.zeros((4, 8, width), f32)
        side[1] = jnp.zeros((3, full, 128), f32)

    @pl.when(jnp.logical_not(band_high))
    def _():
        for c in range(STEPS):
            air[c, :, depth + 1] = jnp.zeros((4, 8, width), f32)
        side[0] = jnp.zeros((3, full, 128), f32)

    @pl.when(jnp.logical_not(both(both(not_first, not_final), both(band_low, band_high))))
    def _():
        @pl.when(jnp.logical_not(not_first))
        def _():
            side[:, :, rows + HALO :] = jnp.zeros((2, 3, HALO, 128), f32)

        @pl.when(jnp.logical_not(not_final))
        def _():
            side[:, :, rows : rows + HALO] = jnp.zeros((2, 3, HALO, 128), f32)

    barrier = pltpu.get_barrier_semaphore()
    for tile_step, condition in ((0, None), (-1, not_first), (1, not_final)):
        for j in range(bands):
            ok = (band != j) if condition is None else condition

            @pl.when(ok)
            def _(tile_step=tile_step, j=j):
                pl.semaphore_signal(
                    barrier, inc=1, device_id=device(tile_step, j), device_id_type=MESH
                )

    row8 = lax.broadcasted_iota(jnp.int32, (8, width), 0)
    total_col = sum(math.exp(-k / LEVELS) for k in range(LEVELS))
    total_prof = sum(math.exp(-2.0 * k / LEVELS) for k in range(LEVELS))
    col_base = f32(0.0)
    prof_base = f32(0.0)
    for j in range(bands):
        here = band == j
        col_base = jnp.where(here, f32(math.exp(-j * depth / LEVELS) / total_col), col_base)
        prof_base = jnp.where(
            here, f32(LEVELS * math.exp(-2.0 * j * depth / LEVELS) / total_prof), prof_base
        )
    col_ratio = math.exp(-1.0 / LEVELS)
    prof_ratio = math.exp(-2.0 / LEVELS)

    def first_air(i, carry):
        weight, total_u, total_v = carry
        for f in range(4):
            air[0, f, i + 1] = air_in[f, i]
        total_u = total_u + weight * air_in[2, i]
        total_v = total_v + weight * air_in[3, i]
        return weight * f32(col_ratio), total_u, total_v

    nothing = jnp.zeros((8, width), f32)
    _, total_u, total_v = lax.fori_loop(0, depth, first_air, (col_base, nothing, nothing))

    def lookup(i, carry):
        at = pl.ds(pl.multiple_of(i * 8, 8), 8)
        kind = class_in[at, :]
        zero = jnp.zeros((8, cols), f32)
        rate, burn, hot, wet = zero, zero, zero, zero
        for k in range(NFUEL):
            same = kind == k
            rate = jnp.where(same, t_rate[k], rate)
            burn = jnp.where(same, t_burn[k], burn)
            hot = jnp.where(same, t_heat[k], hot)
            wet = jnp.where(same, t_moist[k], wet)
        lr[0, at, :cols] = level_in[at, :]
        lr[1, at, :cols] = rate
        lr[2, at, :cols] = ign_in[at, :].astype(f32)
        binv[at, :] = 1.0 / burn
        heat[at, :] = hot
        moist[at, :] = wet
        fuel_out[at, :] = fuel_in[at, :]
        return carry

    lax.fori_loop(0, chunks, lookup, 0)

    expected = (
        bands - 1 + bands * (not_first.astype(jnp.int32) + not_final.astype(jnp.int32))
    )
    pl.semaphore_wait(barrier, expected)

    def send_wind(c, total_u, total_v):
        stacked = jnp.concatenate([total_u, total_v], axis=0)
        row = lax.broadcasted_iota(jnp.int32, (8, 128), 0)
        for j in range(bands):
            shift = (128 // 4 - coarse * j) % width
            window = (pltpu.roll(stacked, shift, 1) if shift else stacked)[:, :128]
            wsend[c, j] = window
            turned = pltpu.roll(window[8:], 4, 0)
            hsend[c, 0, j] = jnp.where(row < 4, window[:8], turned)
            hsend[c, 1, j] = jnp.where(row >= 4, window[:8], turned)

            @pl.when(band == j)
            def _(window=window, j=j):
                wrecv[c, j] = window

        for j in range(bands):
            send(
                band != j,
                wsend.at[c, j],
                wrecv.at[c, band],
                wind_s.at[c, 2, j],
                wind_r.at[c, 2, band],
                device(0, j),
            )
        for way, tile_step, ok in ((0, -1, not_first), (1, 1, not_final)):
            for j in range(bands):
                send(
                    ok,
                    hsend.at[c, way, j],
                    hrecv.at[c, way, band],
                    wind_s.at[c, way, j],
                    wind_r.at[c, way, band],
                    device(tile_step, j),
                )

    def wait_wind(c):
        for j in range(bands):
            receive(band != j, wrecv.at[c, j], wind_r.at[c, 2, j], wind_s.at[c, 2, j], device(0, j))
        for way, tile_step, ok in ((0, 1, not_final), (1, -1, not_first)):
            for j in range(bands):
                receive(
                    ok,
                    hrecv.at[c, way, j],
                    wind_r.at[c, way, j],
                    wind_s.at[c, way, j],
                    device(tile_step, j),
                )

    def send_air(c):
        send(
            not_final,
            air.at[c, :, pl.ds(1, depth), pl.ds(7, 1), :],
            xh.at[c, 0, :, :, pl.ds(7, 1), :],
            halo_s.at[c, 0],
            halo_r.at[c, 0],
            device(1, band),
        )
        send(
            not_first,
            air.at[c, :, pl.ds(1, depth), pl.ds(0, 1), :],
            xh.at[c, 1, :, :, pl.ds(0, 1), :],
            halo_s.at[c, 1],
            halo_r.at[c, 1],
            device(-1, band),
        )
        send(
            band_high,
            air.at[c, :, depth],
            air.at[c, :, 0],
            halo_s.at[c, 2],
            halo_r.at[c, 2],
            device(0, band + 1),
        )
        send(
            band_low,
            air.at[c, :, 1],
            air.at[c, :, depth + 1],
            halo_s.at[c, 3],
            halo_r.at[c, 3],
            device(0, band - 1),
        )

    def wait_air(c):
        receive(
            not_first,
            xh.at[c, 0, :, :, pl.ds(7, 1), :],
            halo_r.at[c, 0],
            halo_s.at[c, 0],
            device(-1, band),
        )
        receive(
            not_final,
            xh.at[c, 1, :, :, pl.ds(0, 1), :],
            halo_r.at[c, 1],
            halo_s.at[c, 1],
            device(1, band),
        )
        receive(band_low, air.at[c, :, 0], halo_r.at[c, 2], halo_s.at[c, 2], device(0, band - 1))
        receive(
            band_high,
            air.at[c, :, depth + 1],
            halo_r.at[c, 3],
            halo_s.at[c, 3],
            device(0, band + 1),
        )

    send_wind(0, total_u, total_v)
    low_rows, high_rows = pl.ds(0, HALO), pl.ds(rows - HALO, HALO)
    own_rows = pl.ds(0, rows)
    from_next, from_last = pl.ds(rows, HALO), pl.ds(rows + HALO, HALO)
    low_cols, high_cols, own_cols = pl.ds(0, 128), pl.ds(cols - 128, 128), pl.ds(0, cols)
    index = 0
    waits = []
    for tile_step in (-1, 0, 1):
        for band_step in (-1, 0, 1):
            if tile_step == 0 and band_step == 0:
                continue
            src_rows = {-1: low_rows, 0: own_rows, 1: high_rows}[tile_step]
            dst_rows = {-1: from_next, 0: own_rows, 1: from_last}[tile_step]
            src_cols = {-1: low_cols, 0: own_cols, 1: high_cols}[band_step]
            if band_step == 0:
                dst = lr.at[:, dst_rows, own_cols]
            else:
                dst = side.at[0 if band_step < 0 else 1, :, dst_rows, :]
            tile_to = {-1: not_first, 0: None, 1: not_final}
            band_to = {-1: band_low, 0: None, 1: band_high}

            def joined(a, b):
                return b if a is None else (a if b is None else both(a, b))

            send(
                joined(tile_to[tile_step], band_to[band_step]),
                lr.at[:, src_rows, src_cols],
                dst,
                fire_s.at[index],
                fire_r.at[index],
                device(tile_step, band + band_step),
            )
            waits.append(
                (
                    joined(tile_to[-tile_step], band_to[-band_step]),
                    dst,
                    fire_r.at[index],
                    fire_s.at[index],
                    device(-tile_step, band - band_step),
                )
            )
            index += 1
    send_air(0)

    def iota(shape, dim):
        return lax.broadcasted_iota(jnp.int32, shape, dim)

    shape = (2 * full, 32)
    line, source = iota(shape, 0), iota(shape, 1)
    field = (line >= full).astype(jnp.int32)
    line = line - full * field
    own = both(
        line < rows,
        both(
            REFINE * (source - 8 * field) <= line,
            line < REFINE * (source - 8 * field) + REFINE,
        ),
    )
    after = both(
        both(line >= rows, line < rows + HALO),
        source == 16 + 4 * field + (line >= rows + REFINE).astype(jnp.int32),
    )
    before = both(
        line >= rows + HALO,
        source == 30 - 4 * field + (line >= rows + 2 * HALO - REFINE).astype(jnp.int32),
    )
    rx[...] = jnp.where(own | after | before, 1.0, 0.0)
    shape = (128, lanes)
    place, line = iota(shape, 0) - 32, iota(shape, 1)
    line = jnp.where(line < cols + 64, line, line - lanes)
    ry[...] = jnp.where(both(REFINE * place <= line, line < REFINE * place + REFINE), 1.0, 0.0)
    shape = (16, 2 * rows)
    place, line = iota(shape, 0), iota(shape, 1)
    sx[...] = jnp.where(both(REFINE * place <= line, line < REFINE * place + REFINE), 1.0, 0.0)
    shape = (cols, 128)
    line, place = iota(shape, 0), iota(shape, 1) - coarse * (band % 2)
    sy[...] = jnp.where(both(REFINE * place <= line, line < REFINE * place + REFINE), 1.0, 0.0)

    for wait in waits:
        receive(*wait)
    lane = iota((full, 128), 1)
    for k in range(3):
        lr[k, :, cols:] = jnp.where(lane < 64, side[0, k], side[1, k])
    lv[0] = lr[0]
    lv[1] = lr[0]

    row_f = iota((8, lanes), 0)
    lane_f = iota((8, lanes), 1)
    low_lane = jnp.where(band_low, -1, 0)
    high_lane = jnp.where(band_high, -1, cols - 1)

    def advance(src, i, fire_step, burn):
        at = pl.ds(pl.multiple_of(i * 8, 8), 8)
        last = pl.ds(pl.multiple_of(((i + all_chunks - 1) % all_chunks) * 8, 8), 8)
        following = pl.ds(pl.multiple_of(((i + 1) % all_chunks) * 8, 8), 8)
        here = lv[src, at, :]
        west = pltpu.roll(jnp.where(row_f == 7, lv[src, last, :], here), 1, 0)
        east = pltpu.roll(jnp.where(row_f == 0, lv[src, following, :], here), 7, 0)
        south = pltpu.roll(here, 1, 1)
        north = pltpu.roll(here, lanes - 1, 1)
        dw, de, ds, dn = here - west, east - here, here - south, north - here
        if burn:
            low_row = jnp.where(both(i == 0, jnp.logical_not(not_first)), 0, -1)
            high_row = jnp.where(both(i == chunks - 1, jnp.logical_not(not_final)), 7, -1)
            dw = jnp.where(row_f == low_row, 0.0, dw)
            de = jnp.where(row_f == high_row, 0.0, de)
        ds = jnp.where(lane_f == low_lane, 0.0, ds)
        dn = jnp.where(lane_f == high_lane, 0.0, dn)
        up_w, up_e = jnp.maximum(dw, 0.0), jnp.minimum(de, 0.0)
        up_s, up_n = jnp.maximum(ds, 0.0), jnp.minimum(dn, 0.0)
        square = (up_w * up_w + up_e * up_e) + (up_s * up_s + up_n * up_n)
        steep = square * lax.rsqrt(jnp.maximum(square, TINY))
        gx, gy = dw + de, ds + dn
        at_v = pl.ds(pl.multiple_of(full + i * 8, 8), 8)
        tail = (wind[at, :] * gx + wind[at_v, :] * gy) * lax.rsqrt(gx * gx + gy * gy + 4.0)
        speed = (fire_step * lr[1, at, :]) * (1.0 + 0.5 * jnp.maximum(tail, 0.0))
        new = here - speed * steep
        lv[1 - src, at, :] = new
        if burn:
            bsum[at, :] = bsum[at, :] + jnp.clip(0.5 - new[:, :cols], 0.0, 1.0)

    lane_a = lax.broadcasted_iota(jnp.int32, (8, width), 1)

    for c in range(STEPS):
        fire_step = plan[c].astype(f32) * f32(0.15)

        def ignite(i, carry):
            at = pl.ds(pl.multiple_of(i * 8, 8), 8)
            now = lv[0, at, :]
            lv[0, at, :] = jnp.where(lr[2, at, :] <= float(c), jnp.minimum(now, -1.0), now)
            return carry

        lax.fori_loop(0, all_chunks, ignite, 0)
        bsum[...] = jnp.zeros_like(bsum)
        wait_wind(c)
        own = wrecv[c, 0]
        after = hrecv[c, 0, 0]
        before = hrecv[c, 1, 0]
        for j in range(1, bands):
            own = own + wrecv[c, j]
            after = after + hrecv[c, 0, j]
            before = before + hrecv[c, 1, j]
        together = jnp.concatenate([own, after, before], axis=0)
        wide = jnp.dot(together, ry[...], precision=HIGH, preferred_element_type=f32)
        wind[...] = jnp.dot(rx[...], wide, precision=HIGH, preferred_element_type=f32)

        near = (SUBSTEPS * (STEPS - c)) > 8

        def pair(k, carry):
            for src in (0, 1):

                def inner(i, carry):
                    advance(src, i, fire_step, True)
                    return carry

                lax.fori_loop(0, chunks, inner, 0)
                if near:

                    def outer(i, carry):
                        advance(src, i, fire_step, False)
                        return carry

                    lax.fori_loop(chunks, all_chunks, outer, 0)
                else:
                    advance(src, chunks, fire_step, False)
                    advance(src, all_chunks - 1, fire_step, False)
            return carry

        lax.fori_loop(0, SUBSTEPS // 2, pair, 0)

        def burn(i, carry):
            at = pl.ds(pl.multiple_of(i * 8, 8), 8)
            fuel = fuel_out[at, :]
            remain = fuel * jnp.exp(-fire_step * bsum[at, :] * binv[at, :])
            used = fuel - remain
            fuel_out[at, :] = remain
            ev[at, :] = used * heat[at, :]
            ev[pl.ds(pl.multiple_of(rows + i * 8, 8), 8), :] = used * moist[at, :]
            return carry

        lax.fori_loop(0, chunks, burn, 0)
        lines = jnp.dot(sx[...], ev[...], precision=HIGH, preferred_element_type=f32)
        flux = jnp.dot(lines, sy[...], precision=HIGH, preferred_element_type=f32)
        flux = flux * f32(1.0 / (REFINE * REFINE))
        fsend[c] = flux
        for j in range(bands):

            @pl.when(band == j)
            def _(j=j):
                frecv[c, j] = flux

            send(
                band != j,
                fsend.at[c],
                frecv.at[c, band],
                flux_s.at[c, j],
                flux_r.at[c, band],
                device(0, j),
            )

        wait_air(c)
        final = c == STEPS - 1

        def write(f, i, value):
            if final:
                air_out[f, i] = value
            else:
                air[c + 1, f, i + 1] = value

        def update(i, carry):
            weight, total_u, total_v = carry
            u, v = air[c, 2, i + 1], air[c, 3, i + 1]
            u_up, u_dn = jnp.maximum(u, 0.0), jnp.minimum(u, 0.0)
            v_up, v_dn = jnp.maximum(v, 0.0), jnp.minimum(v, 0.0)
            lift_x = lift_y = None
            for f in range(4):
                here = air[c, f, i + 1]
                west = pltpu.roll(jnp.where(row8 == 7, xh[c, 0, f, i], here), 1, 0)
                east = pltpu.roll(jnp.where(row8 == 0, xh[c, 1, f, i], here), 7, 0)
                south = jnp.where(lane_a == 0, 0.0, pltpu.roll(here, 1, 1))
                north = jnp.where(lane_a == width - 1, 0.0, pltpu.roll(here, width - 1, 1))
                dw, de, ds, dn = here - west, east - here, here - south, north - here
                advect = u_up * dw + u_dn * de + v_up * ds + v_dn * dn
                lap = (de - dw) + (dn - ds) + (
                    (air[c, f, i] + air[c, f, i + 2]) - 2.0 * here
                )
                new = here + 0.1 * (0.2 * lap - advect)
                if f == 0:
                    lift_x, lift_y = east - west, north - south
                elif f == 1:
                    lift_x = lift_x + 0.6 * (east - west)
                    lift_y = lift_y + 0.6 * (north - south)
                elif f == 2:
                    new = new + 0.015 * lift_x
                    total_u = total_u + weight * new
                else:
                    new = new + 0.015 * lift_y
                    total_v = total_v + weight * new
                write(f, i, new)
            return weight * f32(col_ratio), total_u, total_v

        _, total_u, total_v = lax.fori_loop(0, depth, update, (col_base, nothing, nothing))
        if not final:
            send_wind(c + 1, total_u, total_v)
        for j in range(bands):
            receive(band != j, frecv.at[c, j], flux_r.at[c, j], flux_s.at[c, j], device(0, j))
        parts = [
            frecv[c, 2 * k] + frecv[c, 2 * k + 1] for k in range(width // 128)
        ]
        whole = jnp.concatenate(parts, axis=1)
        heat_in, moist_in = whole[:8], whole[8:]

        def force(i, weight):
            for f, flux in ((0, heat_in), (1, moist_in)):
                now = air_out[f, i] if final else air[c + 1, f, i + 1]
                write(f, i, now + weight * flux)
            return weight * f32(prof_ratio)

        lax.fori_loop(0, depth, force, prof_base * f32(2.0))
        if not final:
            send_air(c + 1)

    level_out[...] = lv[0, :rows, :cols]
    for condition, make in pending:

        @pl.when(condition)
        def _(make=make):
            make().wait_send()


def solution(mesh):
    tiles, sects, subs = (mesh.shape[name] for name in ("tile", "sect", "sub"))
    bands = sects * subs
    air_spec = P(None, ("sect", "sub"), ("group", "tile"), None)
    fire_spec = P(("group", "tile"), ("sect", "sub"))

    def local(air_state, fire_level, *rest):
        depth, width = air_state.shape[1], air_state.shape[3]
        rows, cols = fire_level.shape
        full, lanes = rows + 2 * HALO, cols + 128
        assert air_state.shape[2] == 8 and cols == 64 * REFINE and rows == 8 * REFINE
        vmem = pl.BlockSpec(memory_space=pltpu.VMEM)
        smem = pl.BlockSpec(memory_space=pltpu.SMEM)
        dma = pltpu.SemaphoreType.DMA
        return pl.pallas_call(
            functools.partial(kernel, tiles, sects, subs),
            out_shape=(
                jax.ShapeDtypeStruct(air_state.shape, f32),
                jax.ShapeDtypeStruct(fire_level.shape, f32),
                jax.ShapeDtypeStruct(fire_level.shape, f32),
            ),
            in_specs=[vmem] * 5 + [smem] * 5,
            out_specs=(vmem, vmem, vmem),
            scratch_shapes=[
                pltpu.VMEM((STEPS, 4, depth + 2, 8, width), f32),
                pltpu.VMEM((STEPS, 2, 4, depth, 8, width), f32),
                pltpu.VMEM((3, full, lanes), f32),
                pltpu.VMEM((2, 3, full, 128), f32),
                pltpu.VMEM((2, full, lanes), f32),
                pltpu.VMEM((rows, cols), f32),
                pltpu.VMEM((rows, cols), f32),
                pltpu.VMEM((rows, cols), f32),
                pltpu.VMEM((rows, cols), f32),
                pltpu.VMEM((2 * rows, cols), f32),
                pltpu.VMEM((2 * full, lanes), f32),
                pltpu.VMEM((2 * full, 32), f32),
                pltpu.VMEM((128, lanes), f32),
                pltpu.VMEM((16, 2 * rows), f32),
                pltpu.VMEM((cols, 128), f32),
                pltpu.VMEM((STEPS, bands, 16, 128), f32),
                pltpu.VMEM((STEPS, bands, 16, 128), f32),
                pltpu.VMEM((STEPS, 2, bands, 8, 128), f32),
                pltpu.VMEM((STEPS, 2, bands, 8, 128), f32),
                pltpu.VMEM((STEPS, 16, 128), f32),
                pltpu.VMEM((STEPS, bands, 16, 128), f32),
                dma((8,)),
                dma((8,)),
                dma((STEPS, 3, bands)),
                dma((STEPS, 3, bands)),
                dma((STEPS, bands)),
                dma((STEPS, bands)),
                dma((STEPS, 4)),
                dma((STEPS, 4)),
            ],
            compiler_params=pltpu.CompilerParams(
                collective_id=0, has_side_effects=True, vmem_limit_bytes=56 * 1024 * 1024
            ),
        )(air_state, fire_level, *rest)

    return jax.shard_map(
        local,
        mesh=mesh,
        in_specs=(air_spec, fire_spec, fire_spec, fire_spec, fire_spec) + (P(),) * 5,
        out_specs=(air_spec, fire_spec, fire_spec),
        check_vma=False,
    )
```

time: 525 us -> 68.7 us (0.13)
  the two profiles are of different devices: /device:TPU:9 before, /device:TPU:0 now
where the time goes in v1:
time: 68.7 us; the launch traced here: 68.5 us
  Pallas kernels  64.1 us (93%)
  local copies, waits for them, and re-layouts  3.71 us (5%)
    pallas_call x1, Pallas kernels, local(): pl.pallas_call(functools.partial(kernel, tiles, sects, subs), out_shape=(...  64.1 us
    unnamed x7, local copies, waits for them, and re-layouts  3.71 us

profile of v1, /device:TPU:0, one launch (start us, length us, event | category | flops | bytes accessed | tf_op | source)
XLA Modules:
  0.0 68.5 jit_solution(13425275214759671664)
XLA Ops:
  0.6 64.1 %shard_map.121 = (f32[4,20,8,256]{3,2,1,0:T(8,128)}, f32[80,640]{1,0:T(8,128)}, f32[80,640]{1,0:T(8,128)}) custom-call(f32[4,20,8,256]{3,2,1,0:T(8,128)} %air_in.1, f32[80,640]{1,0:T(8,128)} %level_in.1, f32[80,640]{1,0:T(8,128)} %fuel_in.1, s32[80,640]{1,0:T(8,128)} %class_in.1, s32[80,640]{1,0:T(8,128)} %ign_in.1, s32[4]{0:T(128)} %plan.1, f32[13]{0:T(128)} %t_rate.1, ...), custom_call_target="tpu_custom_call" | custom-call | tf_op jit(solution)/shard_map/pallas_call | solution.py:630
  64.8 0.0 copy-start.1
  64.8 2.0 %copy.16 = f32[4,20,8,256]{3,2,1,0:T(8,128)} copy(f32[4,20,8,256]{3,2,1,0:T(8,128)} %get-tuple-element.6) | data formatting | bytes 1310720
  66.8 0.0 copy-done.1
  66.8 0.0 copy-start
  66.8 0.7 copy.17
  67.5 0.3 copy-done
  67.8 0.7 copy.18
Async XLA Ops:
  64.8 2.0 %copy-start.1 = (f32[80,640]{1,0:T(8,128)S(1)}, f32[80,640]{1,0:T(8,128)}, u32[]{:S(2)}) copy-start(f32[80,640]{1,0:T(8,128)} %get-tuple-element.7) | copy-start | bytes 614404
  66.8 1.0 %copy-start = (f32[80,640]{1,0:T(8,128)S(1)}, f32[80,640]{1,0:T(8,128)}, u32[]{:S(2)}) copy-start(f32[80,640]{1,0:T(8,128)} %get-tuple-element.8) | copy-start | bytes 614404

commit v2 on v1

--- a/solution.py
+++ b/solution.py
@@ -14,10 +14,22 @@
 STEPS = 4
 SUBSTEPS = 4
 HALO = STEPS * SUBSTEPS
-HIGH = lax.Precision.HIGHEST
 MESH = pl.DeviceIdType.MESH
 TINY = 1.1754944e-38
 f32 = jnp.float32
+bf16 = jnp.bfloat16
+
+
+def split(value, axis, pieces):
+    parts = []
+    for _ in range(pieces):
+        parts.append(value.astype(bf16))
+        value = value - parts[-1].astype(f32)
+    return jnp.concatenate(parts, axis=axis)
+
+
+def repeated(mask, axis, pieces):
+    return jnp.concatenate([jnp.where(mask, 1.0, 0.0).astype(bf16)] * pieces, axis=axis)
 
 
 def kernel(
@@ -409,17 +421,17 @@
         line >= rows + HALO,
         source == 30 - 4 * field + (line >= rows + 2 * HALO - REFINE).astype(jnp.int32),
     )
-    rx[...] = jnp.where(own | after | before, 1.0, 0.0)
+    rx[...] = repeated(own | after | before, 1, 3)
     shape = (128, lanes)
     place, line = iota(shape, 0) - 32, iota(shape, 1)
     line = jnp.where(line < cols + 64, line, line - lanes)
-    ry[...] = jnp.where(both(REFINE * place <= line, line < REFINE * place + REFINE), 1.0, 0.0)
+    ry[...] = repeated(both(REFINE * place <= line, line < REFINE * place + REFINE), 0, 2)
     shape = (16, 2 * rows)
     place, line = iota(shape, 0), iota(shape, 1)
-    sx[...] = jnp.where(both(REFINE * place <= line, line < REFINE * place + REFINE), 1.0, 0.0)
+    sx[...] = repeated(both(REFINE * place <= line, line < REFINE * place + REFINE), 1, 3)
     shape = (cols, 128)
     line, place = iota(shape, 0), iota(shape, 1) - coarse * (band % 2)
-    sy[...] = jnp.where(both(REFINE * place <= line, line < REFINE * place + REFINE), 1.0, 0.0)
+    sy[...] = repeated(both(REFINE * place <= line, line < REFINE * place + REFINE), 0, 2)
 
     for wait in waits:
         receive(*wait)
@@ -466,91 +478,15 @@
 
     lane_a = lax.broadcasted_iota(jnp.int32, (8, width), 1)
 
-    for c in range(STEPS):
-        fire_step = plan[c].astype(f32) * f32(0.15)
-
-        def ignite(i, carry):
-            at = pl.ds(pl.multiple_of(i * 8, 8), 8)
-            now = lv[0, at, :]
-            lv[0, at, :] = jnp.where(lr[2, at, :] <= float(c), jnp.minimum(now, -1.0), now)
-            return carry
-
-        lax.fori_loop(0, all_chunks, ignite, 0)
-        bsum[...] = jnp.zeros_like(bsum)
-        wait_wind(c)
-        own = wrecv[c, 0]
-        after = hrecv[c, 0, 0]
-        before = hrecv[c, 1, 0]
-        for j in range(1, bands):
-            own = own + wrecv[c, j]
-            after = after + hrecv[c, 0, j]
-            before = before + hrecv[c, 1, j]
-        together = jnp.concatenate([own, after, before], axis=0)
-        wide = jnp.dot(together, ry[...], precision=HIGH, preferred_element_type=f32)
-        wind[...] = jnp.dot(rx[...], wide, precision=HIGH, preferred_element_type=f32)
-
-        near = (SUBSTEPS * (STEPS - c)) > 8
-
-        def pair(k, carry):
-            for src in (0, 1):
-
-                def inner(i, carry):
-                    advance(src, i, fire_step, True)
-                    return carry
-
-                lax.fori_loop(0, chunks, inner, 0)
-                if near:
-
-                    def outer(i, carry):
-                        advance(src, i, fire_step, False)
-                        return carry
-
-                    lax.fori_loop(chunks, all_chunks, outer, 0)
-                else:
-                    advance(src, chunks, fire_step, False)
-                    advance(src, all_chunks - 1, fire_step, False)
-            return carry
-
-        lax.fori_loop(0, SUBSTEPS // 2, pair, 0)
-
-        def burn(i, carry):
-            at = pl.ds(pl.multiple_of(i * 8, 8), 8)
-            fuel = fuel_out[at, :]
-            remain = fuel * jnp.exp(-fire_step * bsum[at, :] * binv[at, :])
-            used = fuel - remain
-            fuel_out[at, :] = remain
-            ev[at, :] = used * heat[at, :]
-            ev[pl.ds(pl.multiple_of(rows + i * 8, 8), 8), :] = used * moist[at, :]
-            return carry
-
-        lax.fori_loop(0, chunks, burn, 0)
-        lines = jnp.dot(sx[...], ev[...], precision=HIGH, preferred_element_type=f32)
-        flux = jnp.dot(lines, sy[...], precision=HIGH, preferred_element_type=f32)
-        flux = flux * f32(1.0 / (REFINE * REFINE))
-        fsend[c] = flux
-        for j in range(bands):
-
-            @pl.when(band == j)
-            def _(j=j):
-                frecv[c, j] = flux
-
-            send(
-                band != j,
-                fsend.at[c],
-                frecv.at[c, band],
-                flux_s.at[c, j],
-                flux_r.at[c, band],
-                device(0, j),
-            )
-
+    def write(c, f, i, value):
+        if c == STEPS - 1:
+            air_out[f, i] = value
+        else:
+            air[c + 1, f, i + 1] = value
+
+    def move_air(c):
         wait_air(c)
         final = c == STEPS - 1
-
-        def write(f, i, value):
-            if final:
-                air_out[f, i] = value
-            else:
-                air[c + 1, f, i + 1] = value
 
         def update(i, carry):
             weight, total_u, total_v = carry
@@ -581,12 +517,15 @@
                 else:
                     new = new + 0.015 * lift_y
                     total_v = total_v + weight * new
-                write(f, i, new)
+                write(c, f, i, new)
             return weight * f32(col_ratio), total_u, total_v
 
-        _, total_u, total_v = lax.fori_loop(0, depth, update, (col_base, nothing, nothing))
+        _, total_u, total_v = lax.fori_loop(0, depth, update, (col_base, nothing, nothing), unroll=2)
         if not final:
             send_wind(c + 1, total_u, total_v)
+
+    def finish_air(c):
+        final = c == STEPS - 1
         for j in range(bands):
             receive(band != j, frecv.at[c, j], flux_r.at[c, j], flux_s.at[c, j], device(0, j))
         parts = [
@@ -598,13 +537,93 @@
         def force(i, weight):
             for f, flux in ((0, heat_in), (1, moist_in)):
                 now = air_out[f, i] if final else air[c + 1, f, i + 1]
-                write(f, i, now + weight * flux)
+                write(c, f, i, now + weight * flux)
             return weight * f32(prof_ratio)
 
-        lax.fori_loop(0, depth, force, prof_base * f32(2.0))
-        if not final:
-            send_air(c + 1)
-
+        lax.fori_loop(0, depth, force, prof_base * f32(2.0), unroll=2)
+
+    for c in range(STEPS):
+        fire_step = plan[c].astype(f32) * f32(0.15)
+
+        def ignite(i, carry):
+            at = pl.ds(pl.multiple_of(i * 8, 8), 8)
+            now = lv[0, at, :]
+            lv[0, at, :] = jnp.where(lr[2, at, :] <= float(c), jnp.minimum(now, -1.0), now)
+            return carry
+
+        lax.fori_loop(0, all_chunks, ignite, 0)
+        bsum[...] = jnp.zeros_like(bsum)
+        wait_wind(c)
+        own = wrecv[c, 0]
+        after = hrecv[c, 0, 0]
+        before = hrecv[c, 1, 0]
+        for j in range(1, bands):
+            own = own + wrecv[c, j]
+            after = after + hrecv[c, 0, j]
+            before = before + hrecv[c, 1, j]
+        together = jnp.concatenate([own, after, before], axis=0)
+        wide = jnp.dot(split(together, 1, 2), ry[...], preferred_element_type=f32)
+        wind[...] = jnp.dot(rx[...], split(wide, 0, 3), preferred_element_type=f32)
+
+        near = (SUBSTEPS * (STEPS - c)) > 8
+
+        def substep(src, fire_step=fire_step, near=near):
+            def inner(i, carry):
+                advance(src, i, fire_step, True)
+                return carry
+
+            lax.fori_loop(0, chunks, inner, 0, unroll=5)
+            if near:
+
+                def outer(i, carry):
+                    advance(src, i, fire_step, False)
+                    return carry
+
+                lax.fori_loop(chunks, all_chunks, outer, 0, unroll=2)
+            else:
+                advance(src, chunks, fire_step, False)
+                advance(src, all_chunks - 1, fire_step, False)
+
+        substep(0)
+        if c > 0:
+            finish_air(c - 1)
+            send_air(c)
+        substep(1)
+        substep(0)
+        move_air(c)
+        substep(1)
+
+        def burn(i, carry):
+            at = pl.ds(pl.multiple_of(i * 8, 8), 8)
+            fuel = fuel_out[at, :]
+            remain = fuel * jnp.exp(-fire_step * bsum[at, :] * binv[at, :])
+            used = fuel - remain
+            fuel_out[at, :] = remain
+            ev[at, :] = used * heat[at, :]
+            ev[pl.ds(pl.multiple_of(rows + i * 8, 8), 8), :] = used * moist[at, :]
+            return carry
+
+        lax.fori_loop(0, chunks, burn, 0)
+        lines = jnp.dot(split(ev[...], 1, 2), sy[...], preferred_element_type=f32)
+        flux = jnp.dot(sx[...], split(lines, 0, 3), preferred_element_type=f32)
+        flux = flux * f32(1.0 / (REFINE * REFINE))
+        fsend[c] = flux
+        for j in range(bands):
+
+            @pl.when(band == j)
+            def _(j=j):
+                frecv[c, j] = flux
+
+            send(
+                band != j,
+                fsend.at[c],
+                frecv.at[c, band],
+                flux_s.at[c, j],
+                flux_r.at[c, band],
+                device(0, j),
+            )
+
+    finish_air(STEPS - 1)
     level_out[...] = lv[0, :rows, :cols]
     for condition, make in pending:
 
@@ -648,10 +667,10 @@
                 pltpu.VMEM((rows, cols), f32),
                 pltpu.VMEM((2 * rows, cols), f32),
                 pltpu.VMEM((2 * full, lanes), f32),
-                pltpu.VMEM((2 * full, 32), f32),
-                pltpu.VMEM((128, lanes), f32),
-                pltpu.VMEM((16, 2 * rows), f32),
-                pltpu.VMEM((cols, 128), f32),
+                pltpu.VMEM((2 * full, 96), bf16),
+                pltpu.VMEM((256, lanes), bf16),
+                pltpu.VMEM((16, 6 * rows), bf16),
+                pltpu.VMEM((2 * cols, 128), bf16),
                 pltpu.VMEM((STEPS, bands, 16, 128), f32),
                 pltpu.VMEM((STEPS, bands, 16, 128), f32),
                 pltpu.VMEM((STEPS, 2, bands, 8, 128), f32),

time: 68.7 us -> 60.9 us (0.89)
  Pallas kernels: 64.1 us -> 56.3 us
    pallas_call x1, Pallas kernels: 64.1 us -> 56.3 us  [local(): pl.pallas_call(functools.partial(kernel, tiles, sects, subs), out_shape=(...]
where the time goes in v2:
time: 60.9 us; the launch traced here: 60.7 us
  Pallas kernels  56.3 us (92%)
  local copies, waits for them, and re-layouts  3.71 us (6%)
  between operations  0.65 us (1%)
    pallas_call x1, Pallas kernels, local(): pl.pallas_call(functools.partial(kernel, tiles, sects, subs), out_shape=(...  56.3 us
    unnamed x7, local copies, waits for them, and re-layouts  3.71 us

profile of v2, /device:TPU:0, one launch (start us, length us, event | category | flops | bytes accessed | tf_op | source)
XLA Modules:
  0.0 60.7 jit_solution(8560456379563905864)
XLA Ops:
  0.6 56.3 %shard_map.121 = (f32[4,20,8,256]{3,2,1,0:T(8,128)}, f32[80,640]{1,0:T(8,128)}, f32[80,640]{1,0:T(8,128)}) custom-call(f32[4,20,8,256]{3,2,1,0:T(8,128)} %air_in.1, f32[80,640]{1,0:T(8,128)} %level_in.1, f32[80,640]{1,0:T(8,128)} %fuel_in.1, s32[80,640]{1,0:T(8,128)} %class_in.1, s32[80,640]{1,0:T(8,128)} %ign_in.1, s32[4]{0:T(128)} %plan.1, f32[13]{0:T(128)} %t_rate.1, ...), custom_call_target="tpu_custom_call" | custom-call | tf_op jit(solution)/shard_map/pallas_call | solution.py:649
  57.0 0.0 copy-start.1
  57.0 2.0 %copy.16 = f32[4,20,8,256]{3,2,1,0:T(8,128)} copy(f32[4,20,8,256]{3,2,1,0:T(8,128)} %get-tuple-element.6) | data formatting | bytes 1310720
  59.0 0.0 copy-done.1
  59.0 0.0 copy-start
  59.0 0.7 %copy.17 = f32[80,640]{1,0:T(8,128)} copy(f32[80,640]{1,0:T(8,128)S(1)} %copy-done.1) | data formatting | bytes 409600
  59.7 0.3 copy-done
  60.0 0.7 %copy.18 = f32[80,640]{1,0:T(8,128)} copy(f32[80,640]{1,0:T(8,128)S(1)} %copy-done) | data formatting | bytes 409600
Async XLA Ops:
  57.0 2.0 %copy-start.1 = (f32[80,640]{1,0:T(8,128)S(1)}, f32[80,640]{1,0:T(8,128)}, u32[]{:S(2)}) copy-start(f32[80,640]{1,0:T(8,128)} %get-tuple-element.7) | copy-start | bytes 614404
  59.0 1.0 %copy-start = (f32[80,640]{1,0:T(8,128)S(1)}, f32[80,640]{1,0:T(8,128)}, u32[]{:S(2)}) copy-start(f32[80,640]{1,0:T(8,128)} %get-tuple-element.8) | copy-start | bytes 614404

commit v3 on v2

--- a/solution.py
+++ b/solution.py
@@ -585,12 +585,13 @@
                 advance(src, all_chunks - 1, fire_step, False)
 
         substep(0)
-        if c > 0:
+        substep(1)
+        if c % 2 == 0:
+            move_air(c)
+        else:
             finish_air(c - 1)
             send_air(c)
-        substep(1)
         substep(0)
-        move_air(c)
         substep(1)
 
         def burn(i, carry):
@@ -622,8 +623,12 @@
                 flux_r.at[c, band],
                 device(0, j),
             )
-
-    finish_air(STEPS - 1)
+        if c % 2 == 1:
+            move_air(c)
+            finish_air(c)
+            if c < STEPS - 1:
+                send_air(c + 1)
+
     level_out[...] = lv[0, :rows, :cols]
     for condition, make in pending:
 

time: 60.9 us -> 56.8 us (0.933)
  Pallas kernels: 56.3 us -> 52.2 us
    pallas_call x1, Pallas kernels: 56.3 us -> 52.2 us  [local(): pl.pallas_call(functools.partial(kernel, tiles, sects, subs), out_shape=(...]
where the time goes in v3:
time: 56.8 us; the launch traced here: 56.6 us
  Pallas kernels  52.2 us (92%)
  local copies, waits for them, and re-layouts  3.71 us (7%)
  between operations  0.65 us (1%)
    pallas_call x1, Pallas kernels, local(): pl.pallas_call(functools.partial(kernel, tiles, sects, subs), out_shape=(...  52.2 us
    unnamed x7, local copies, waits for them, and re-layouts  3.71 us

profile of v3, /device:TPU:0, one launch (start us, length us, event | category | flops | bytes accessed | tf_op | source)
XLA Modules:
  0.0 56.6 jit_solution(4888075117692060895)
XLA Ops:
  0.6 52.2 %shard_map.121 = (f32[4,20,8,256]{3,2,1,0:T(8,128)}, f32[80,640]{1,0:T(8,128)}, f32[80,640]{1,0:T(8,128)}) custom-call(f32[4,20,8,256]{3,2,1,0:T(8,128)} %air_in.1, f32[80,640]{1,0:T(8,128)} %level_in.1, f32[80,640]{1,0:T(8,128)} %fuel_in.1, s32[80,640]{1,0:T(8,128)} %class_in.1, s32[80,640]{1,0:T(8,128)} %ign_in.1, s32[4]{0:T(128)} %plan.1, f32[13]{0:T(128)} %t_rate.1, ...), custom_call_target="tpu_custom_call" | custom-call | tf_op jit(solution)/shard_map/pallas_call | solution.py:654
  52.9 0.0 copy-start.1
  52.9 2.0 %copy.16 = f32[4,20,8,256]{3,2,1,0:T(8,128)} copy(f32[4,20,8,256]{3,2,1,0:T(8,128)} %get-tuple-element.6) | data formatting | bytes 1310720
  54.9 0.0 copy-done.1
  54.9 0.0 copy-start
  54.9 0.7 %copy.17 = f32[80,640]{1,0:T(8,128)} copy(f32[80,640]{1,0:T(8,128)S(1)} %copy-done.1) | data formatting | bytes 409600
  55.6 0.3 copy-done
  55.9 0.7 %copy.18 = f32[80,640]{1,0:T(8,128)} copy(f32[80,640]{1,0:T(8,128)S(1)} %copy-done) | data formatting | bytes 409600
Async XLA Ops:
  52.9 2.0 %copy-start.1 = (f32[80,640]{1,0:T(8,128)S(1)}, f32[80,640]{1,0:T(8,128)}, u32[]{:S(2)}) copy-start(f32[80,640]{1,0:T(8,128)} %get-tuple-element.7) | copy-start | bytes 614404
  54.9 1.0 %copy-start = (f32[80,640]{1,0:T(8,128)S(1)}, f32[80,640]{1,0:T(8,128)}, u32[]{:S(2)}) copy-start(f32[80,640]{1,0:T(8,128)} %get-tuple-element.8) | copy-start | bytes 614404

commit v4 on v3

--- a/solution.py
+++ b/solution.py
@@ -356,6 +356,7 @@
         )
 
     send_wind(0, total_u, total_v)
+    send_air(0)
     low_rows, high_rows = pl.ds(0, HALO), pl.ds(rows - HALO, HALO)
     own_rows = pl.ds(0, rows)
     from_next, from_last = pl.ds(rows, HALO), pl.ds(rows + HALO, HALO)
@@ -397,7 +398,6 @@
                 )
             )
             index += 1
-    send_air(0)
 
     def iota(shape, dim):
         return lax.broadcasted_iota(jnp.int32, shape, dim)
@@ -432,14 +432,6 @@
     shape = (cols, 128)
     line, place = iota(shape, 0), iota(shape, 1) - coarse * (band % 2)
     sy[...] = repeated(both(REFINE * place <= line, line < REFINE * place + REFINE), 0, 2)
-
-    for wait in waits:
-        receive(*wait)
-    lane = iota((full, 128), 1)
-    for k in range(3):
-        lr[k, :, cols:] = jnp.where(lane < 64, side[0, k], side[1, k])
-    lv[0] = lr[0]
-    lv[1] = lr[0]
 
     row_f = iota((8, lanes), 0)
     lane_f = iota((8, lanes), 1)
@@ -542,6 +534,15 @@
 
         lax.fori_loop(0, depth, force, prof_base * f32(2.0), unroll=2)
 
+    move_air(0)
+    for wait in waits:
+        receive(*wait)
+    lane = iota((full, 128), 1)
+    for k in range(3):
+        lr[k, :, cols:] = jnp.where(lane < 64, side[0, k], side[1, k])
+    lv[0] = lr[0]
+    lv[1] = lr[0]
+
     for c in range(STEPS):
         fire_step = plan[c].astype(f32) * f32(0.15)
 
@@ -586,9 +587,9 @@
 
         substep(0)
         substep(1)
-        if c % 2 == 0:
+        if c % 2 == 0 and c > 0:
             move_air(c)
-        else:
+        elif c % 2 == 1:
             finish_air(c - 1)
             send_air(c)
         substep(0)

time: 56.8 us -> 56.9 us (level)
  no operation moved by 1% of the time
where the time goes in v4:
time: 56.9 us; the launch traced here: 56.7 us
  Pallas kernels  52.3 us (92%)
  local copies, waits for them, and re-layouts  3.71 us (7%)
  between operations  0.65 us (1%)
    pallas_call x1, Pallas kernels, local(): pl.pallas_call(functools.partial(kernel, tiles, sects, subs), out_shape=(...  52.3 us
    unnamed x7, local copies, waits for them, and re-layouts  3.71 us

profile of v4, /device:TPU:0, one launch (start us, length us, event | category | flops | bytes accessed | tf_op | source)
XLA Modules:
  0.0 56.7 jit_solution(16068112447484297741)
XLA Ops:
  0.6 52.3 %shard_map.121 = (f32[4,20,8,256]{3,2,1,0:T(8,128)}, f32[80,640]{1,0:T(8,128)}, f32[80,640]{1,0:T(8,128)}) custom-call(f32[4,20,8,256]{3,2,1,0:T(8,128)} %air_in.1, f32[80,640]{1,0:T(8,128)} %level_in.1, f32[80,640]{1,0:T(8,128)} %fuel_in.1, s32[80,640]{1,0:T(8,128)} %class_in.1, s32[80,640]{1,0:T(8,128)} %ign_in.1, s32[4]{0:T(128)} %plan.1, f32[13]{0:T(128)} %t_rate.1, ...), custom_call_target="tpu_custom_call" | custom-call | tf_op jit(solution)/shard_map/pallas_call | solution.py:655
  52.9 0.0 copy-start.1
  53.0 2.0 %copy.16 = f32[4,20,8,256]{3,2,1,0:T(8,128)} copy(f32[4,20,8,256]{3,2,1,0:T(8,128)} %get-tuple-element.6) | data formatting | bytes 1310720
  55.0 0.0 copy-done.1
  55.0 0.0 copy-start
  55.0 0.7 %copy.17 = f32[80,640]{1,0:T(8,128)} copy(f32[80,640]{1,0:T(8,128)S(1)} %copy-done.1) | data formatting | bytes 409600
  55.7 0.3 copy-done
  56.0 0.7 %copy.18 = f32[80,640]{1,0:T(8,128)} copy(f32[80,640]{1,0:T(8,128)S(1)} %copy-done) | data formatting | bytes 409600
Async XLA Ops:
  52.9 2.0 %copy-start.1 = (f32[80,640]{1,0:T(8,128)S(1)}, f32[80,640]{1,0:T(8,128)}, u32[]{:S(2)}) copy-start(f32[80,640]{1,0:T(8,128)} %get-tuple-element.7) | copy-start | bytes 614404
  55.0 1.0 %copy-start = (f32[80,640]{1,0:T(8,128)S(1)}, f32[80,640]{1,0:T(8,128)}, u32[]{:S(2)}) copy-start(f32[80,640]{1,0:T(8,128)} %get-tuple-element.8) | copy-start | bytes 614404
